TPU v7x, 32 devices: a whole 2x2x4 slice. The times are simulated.
32 devices in a mesh: snap: 2 (over y), row: 4 (over z), col: 4 (over x, core).
Axes of the slice: x: 2, y: 2, z: 4, core: 2. Of those that a mesh axis runs over, the one named last changes fastest.
Arguments:
- orbitals: float32 [12288, 768], P(('snap', 'row', 'col')), parts along dimension 0, may hold values from -6 to 6
- screened: float32 [6, 6144, 6144], P('snap', 'row', 'col'), parts along dimension 0, may hold values from -0.0029296875 to 0.0029296875
- green_weight: float32 [6, 768], P('snap'), parts along dimension 0, may hold values from 0.05 to 1
- time_weight: float32 [3], replicated, may hold values from 0.3 to 1
Outputs:
- updated: float32 [12288, 768], P(('snap', 'row', 'col')), parts along dimension 0
There are 2 independent parts, one for each index of `snap`. A program takes and returns all parts, laid end to end along the dimension named above; an argument that names none is the same for every part. Nothing has to cross between parts.
All inputs are finite; a program needn't handle non-finite values.
Results may differ from a plain program's by a relative error of at most 0.00013.
Values sent between devices are 32-bit elements; how exact they have to be, the bound alone decides.
A program may use at most 128 MiB of HBM per device.

v0:
```python
import jax
import jax.numpy as jnp
from jax import lax
from jax.sharding import PartitionSpec as P

TIMES = 3
PASSES = 2


def from_root(block, axis, owner):
    block = jnp.where(lax.axis_index(axis) == owner, block, jnp.zeros_like(block))
    return lax.psum(block, axis)


def gather_rows(shard):
    return lax.all_gather(shard, "col", axis=0, tiled=True)


def scatter_rows(partial_value):
    return lax.psum_scatter(partial_value, "col", scatter_dimension=0, tiled=True)


def body(orbitals, screened, green_weight, time_weight):
    n_row = lax.axis_size("row")
    n_col = lax.axis_size("col")
    factor = n_col // n_row
    col_width = screened.shape[2]
    col_index = lax.axis_index("col")
    root = col_index // factor
    offset = col_index % factor * col_width
    own = orbitals
    rows = gather_rows(own)
    for step in range(PASSES):
        piece = lax.dynamic_slice_in_dim(rows, offset, col_width, 0)
        columns = from_root(piece, "row", root)
        partial_value = jnp.zeros(rows.shape, jnp.float32)
        for t in range(TIMES):
            green = lax.dot_general(
                rows * green_weight[t],
                columns,
                (((1,), (1,)), ((), ())),
                precision=lax.Precision.HIGHEST,
                preferred_element_type=jnp.float32,
            )
            applied = jnp.dot(
                green * screened[t],
                columns,
                precision=lax.Precision.HIGHEST,
                preferred_element_type=jnp.float32,
            )
            partial_value = partial_value + time_weight[t] * applied
        final = step == PASSES - 1
        own = own - scatter_rows(partial_value)
        if not final:
            rows = gather_rows(own)
    return own


def solution(mesh):
    in_specs = (P(("snap", "row", "col"), None), P("snap", "row", "col"), P("snap", None), P())
    out_specs = P(("snap", "row", "col"), None)
    return jax.shard_map(body, mesh=mesh, in_specs=in_specs, out_specs=out_specs, check_vma=False)
```

profile of v0, /device:TPU:0, one launch (start us, length us, event | category | flops | bytes accessed | tf_op | source)
XLA Modules:
  0.0 877.8 jit_solution(2341078948588468849)
XLA Ops:
  6.5 0.7 all-gather.3.cloned.1.call-update
  7.3 41.8 %all-gather.3.cloned.1.call-done = f32[1536,768]{1,0:T(8,128)} async-done(((f32[384,768]{1,0:T(8,128)}), f32[1536,768]{1,0:T(8,128)}) %all-gather.3.cloned.1.call-update) | async-done | bytes 4718608 | tf_op jit(solution)/shard_map/all_gather | solution.py:16
  49.1 4.8 broadcast_select_fusion.1
  54.5 0.6 fusion.12
  55.2 170.7 %all-reduce.3.cloned.1.call-done = f32[1536,768]{1,0:T(8,128)} async-done(((f32[1536,768]{1,0:T(8,128)}), f32[1536,768]{1,0:T(8,128)}) %all-reduce.3.cloned.1.call-update) | async-done | bytes 4718608 | tf_op jit(solution)/shard_map/psum | solution.py:12
  225.9 28.3 %convolution_multiply_fusion.4 = f32[1536,1536]{1,0:T(8,128)} fusion(f32[1536,768]{1,0:T(8,128)} %all-reduce.3.cloned.1.call-done, f32[3,1536,1536]{2,1,0:T(8,128)} %param.5, f32[1536,768]{1,0:T(8,128)} %all-gather.3.cloned.1.call-done, f32[768]{0:T(1024)S(1)} %get-tuple-element.7), kind=kOutput, calls=%fused_computation.4 | convolution fusion | flops 21746810880 | bytes 28314624 | tf_op jit(solution)/shard_map/dot_general | solution.py:38
  254.2 28.0 %fusion.14 = f32[1536,768]{1,0:T(8,128)} fusion(f32[1536,1536]{1,0:T(8,128)} %convolution_multiply_fusion.4, f32[1536,768]{1,0:T(8,128)} %all-reduce.3.cloned.1.call-done), kind=kOutput, calls=%fused_computation.27 | convolution fusion | flops 21743271936 | bytes 18874368 | tf_op jit(solution)/shard_map/dot_general | solution.py:45
  282.2 26.8 %convolution_multiply_fusion.5 = f32[1536,1536]{1,0:T(8,128)} fusion(f32[1536,768]{1,0:T(8,128)} %all-reduce.3.cloned.1.call-done, f32[3,1536,1536]{2,1,0:T(8,128)S(1)} %bitcast.31, f32[1536,768]{1,0:T(8,128)S(1)} %bitcast.33, f32[768]{0:T(1024)S(1)} %get-tuple-element.6), kind=kOutput, calls=%fused_computation.5 | convolution fusion | flops 21746810880 | bytes 28314624 | tf_op jit(solution)/shard_map/dot_general | solution.py:38
  309.0 27.7 %fusion.13 = f32[1536,768]{1,0:T(8,128)} fusion(f32[1536,1536]{1,0:T(8,128)} %convolution_multiply_fusion.5, f32[1536,768]{1,0:T(8,128)} %all-reduce.3.cloned.1.call-done), kind=kOutput, calls=%fused_computation.26 | convolution fusion | flops 21743271936 | bytes 18874368 | tf_op jit(solution)/shard_map/dot_general | solution.py:45
  336.8 27.0 %convolution_multiply_fusion.3 = f32[1536,1536]{1,0:T(8,128)} fusion(f32[1536,768]{1,0:T(8,128)} %all-reduce.3.cloned.1.call-done, f32[3,1536,1536]{2,1,0:T(8,128)S(1)} %bitcast.31, f32[1536,768]{1,0:T(8,128)S(1)} %bitcast.33, f32[768]{0:T(1024)S(1)} %get-tuple-element.5), kind=kOutput, calls=%fused_computation.3 | convolution fusion | flops 21746810880 | bytes 28314624 | tf_op jit(solution)/shard_map/dot_general | solution.py:38
  363.8 31.6 %multiply_add_fusion.1 = f32[1536,768]{1,0:T(8,128)} fusion(f32[1536,768]{1,0:T(8,128)} %fusion.14, f32[1536,768]{1,0:T(8,128)} %fusion.13, f32[1536,1536]{1,0:T(8,128)} %convolution_multiply_fusion.3, f32[1536,768]{1,0:T(8,128)} %all-reduce.3.cloned.1.call-done, f32[]{:T(128)} %bitcast.4, f32[]{:T(128)} %bitcast.2, f32[]{:T(128)} %bitcast), kind=kOutput, calls=%fused_computation.10 | convolution fusion | flops 21749170176 | bytes 28311564 | tf_op jit(solution)/shard_map/dot_general | solution.py:45
  395.5 47.0 %reduce-scatter.3.cloned.1.call-done = f32[384,768]{1,0:T(8,128)} async-done(((f32[1536,768]{1,0:T(8,128)}), f32[384,768]{1,0:T(8,128)}) %reduce-scatter.3.cloned.1.call-update) | async-done | bytes 1179664 | tf_op jit(solution)/shard_map/reduce_scatter | solution.py:20
  442.5 2.4 sub.8
  445.0 37.5 %all-gather.5.cloned.1.call-done = f32[1536,768]{1,0:T(8,128)} async-done(((f32[384,768]{1,0:T(8,128)}), f32[1536,768]{1,0:T(8,128)}) %all-gather.5.cloned.1.call-update) | async-done | bytes 4718608 | tf_op jit(solution)/shard_map/all_gather | solution.py:16
  482.5 4.8 broadcast_select_fusion
  487.5 171.9 %all-reduce.5.cloned.1.call-done = f32[1536,768]{1,0:T(8,128)} async-done(((f32[1536,768]{1,0:T(8,128)}), f32[1536,768]{1,0:T(8,128)}) %all-reduce.5.cloned.1.call-update) | async-done | bytes 4718608 | tf_op jit(solution)/shard_map/psum | solution.py:12
  659.4 27.4 %convolution_multiply_fusion.1 = f32[1536,1536]{1,0:T(8,128)S(1)} fusion(f32[1536,768]{1,0:T(8,128)} %all-reduce.5.cloned.1.call-done, f32[3,1536,1536]{2,1,0:T(8,128)} %param.5, f32[1536,768]{1,0:T(8,128)} %all-gather.5.cloned.1.call-done, f32[768]{0:T(1024)S(1)} %get-tuple-element.7), kind=kOutput, calls=%fused_computation.1 | convolution fusion | flops 21746810880 | bytes 28314624 | tf_op jit(solution)/shard_map/dot_general | solution.py:38
  686.8 27.3 %convolution_multiply_fusion.2 = f32[1536,1536]{1,0:T(8,128)} fusion(f32[1536,768]{1,0:T(8,128)S(1)} %copy-done, f32[3,1536,1536]{2,1,0:T(8,128)} %param.5, f32[1536,768]{1,0:T(8,128)} %all-gather.5.cloned.1.call-done, f32[768]{0:T(1024)S(1)} %get-tuple-element.6), kind=kOutput, calls=%fused_computation.2 | convolution fusion | flops 21746810880 | bytes 28314624 | tf_op jit(solution)/shard_map/dot_general | solution.py:38
  714.2 28.4 %convolution_multiply_fusion = f32[1536,1536]{1,0:T(8,128)S(1)} fusion(f32[1536,768]{1,0:T(8,128)S(1)} %copy-done, f32[3,1536,1536]{2,1,0:T(8,128)} %param.5, f32[1536,768]{1,0:T(8,128)S(1)} %bitcast.35, f32[768]{0:T(1024)S(1)} %get-tuple-element.5), kind=kOutput, calls=%fused_computation | convolution fusion | flops 21746810880 | bytes 28314624 | tf_op jit(solution)/shard_map/dot_general | solution.py:38
  742.6 23.3 %fusion.16 = f32[1536,768]{1,0:T(8,128)S(1)} fusion(f32[1536,1536]{1,0:T(8,128)S(1)} %convolution_multiply_fusion.1, f32[1536,768]{1,0:T(8,128)S(1)} %copy-done), kind=kOutput, calls=%fused_computation.29 | convolution fusion | flops 21743271936 | bytes 18874368 | tf_op jit(solution)/shard_map/dot_general | solution.py:45
  765.9 28.4 %fusion.15 = f32[1536,768]{1,0:T(8,128)S(1)} fusion(f32[1536,1536]{1,0:T(8,128)} %convolution_multiply_fusion.2, f32[1536,768]{1,0:T(8,128)S(1)} %copy-done), kind=kOutput, calls=%fused_computation.28 | convolution fusion | flops 21743271936 | bytes 18874368 | tf_op jit(solution)/shard_map/dot_general | solution.py:45
  794.2 27.0 %multiply_add_fusion = f32[1536,768]{1,0:T(8,128)} fusion(f32[1536,768]{1,0:T(8,128)S(1)} %fusion.16, f32[1536,768]{1,0:T(8,128)S(1)} %fusion.15, f32[1536,1536]{1,0:T(8,128)S(1)} %convolution_multiply_fusion, f32[1536,768]{1,0:T(8,128)S(1)} %copy-done, f32[]{:T(128)} %bitcast.4, f32[]{:T(128)} %bitcast.2, f32[]{:T(128)} %bitcast), kind=kOutput, calls=%fused_computation.6 | convolution fusion | flops 21749170176 | bytes 28311564 | tf_op jit(solution)/shard_map/dot_general | solution.py:45
  821.2 47.1 %reduce-scatter.5.cloned.1.call-done = f32[384,768]{1,0:T(8,128)} async-done(((f32[1536,768]{1,0:T(8,128)}), f32[384,768]{1,0:T(8,128)}) %reduce-scatter.5.cloned.1.call-update) | async-done | bytes 1179664 | tf_op jit(solution)/shard_map/reduce_scatter | solution.py:20
  868.3 2.4 sub.9
  (47 shorter events, 1.0 us)
Async XLA Ops:
  6.5 42.5 %all-gather.3.cloned.1.call-start = ((), (), s32[]{:S(2)}) async-start(), calls=%async_computation.2 | async-start | bytes 5898240 | tf_op jit(solution)/shard_map/all_gather | solution.py:16
  7.3 218.6 %all-reduce.3.cloned.1.call-start = ((), (), s32[]{:S(2)}) async-start(), calls=%async_computation.3 | async-start | bytes 9437184 | tf_op jit(solution)/shard_map/psum | solution.py:12
  53.9 0.7 copy-start.4
  53.9 1.3 copy-start.3
  53.9 228.3 %slice-start.7 = ((s8[4718592]{0:T(1024)(128)(4,1)}), s8[524288]{0:T(1024)(128)(4,1)S(1)}, s32[]{:S(2)}) async-start(s8[4718592]{0:T(1024)(128)(4,1)} %bitcast.32), calls=%async_computation.15 | async-start | bytes 1048576
  53.9 388.6 %reduce-scatter.3.cloned.1.call-start = ((), (), s32[]{:S(2)}) async-start(), calls=%async_computation.4 | async-start | bytes 5898240 | tf_op jit(solution)/shard_map/reduce_scatter | solution.py:20
  225.9 56.3 %slice-start = ((s8[28311552]{0:T(1024)(128)(4,1)}), s8[4194304]{0:T(1024)(128)(4,1)S(1)}, s32[]{:S(2)}) async-start(s8[28311552]{0:T(1024)(128)(4,1)} %bitcast.30), calls=%async_computation.8 | async-start | bytes 8388608
  225.9 56.3 %slice-start.1 = ((s8[28311552]{0:T(1024)(128)(4,1)}), s8[4194304]{0:T(1024)(128)(4,1)S(1)}, s32[]{:S(2)}) async-start(s8[28311552]{0:T(1024)(128)(4,1)} %bitcast.30), calls=%async_computation.9 | async-start | bytes 8388608
  225.9 56.3 %slice-start.2 = ((s8[28311552]{0:T(1024)(128)(4,1)}), s8[4194304]{0:T(1024)(128)(4,1)S(1)}, s32[]{:S(2)}) async-start(s8[28311552]{0:T(1024)(128)(4,1)} %bitcast.30), calls=%async_computation.10 | async-start | bytes 8388608
  225.9 56.3 %slice-start.3 = ((s8[28311552]{0:T(1024)(128)(4,1)}), s8[4194304]{0:T(1024)(128)(4,1)S(1)}, s32[]{:S(2)}) async-start(s8[28311552]{0:T(1024)(128)(4,1)} %bitcast.30), calls=%async_computation.11 | async-start | bytes 8388608
  225.9 56.3 %slice-start.8 = ((s8[4718592]{0:T(1024)(128)(4,1)}), s8[4194304]{0:T(1024)(128)(4,1)S(1)}, s32[]{:S(2)}) async-start(s8[4718592]{0:T(1024)(128)(4,1)} %bitcast.32), calls=%async_computation.16 | async-start | bytes 8388608
  254.1 28.0 %slice-start.4 = ((s8[28311552]{0:T(1024)(128)(4,1)}), s8[4194304]{0:T(1024)(128)(4,1)S(1)}, s32[]{:S(2)}) async-start(s8[28311552]{0:T(1024)(128)(4,1)} %bitcast.30), calls=%async_computation.12 | async-start | bytes 8388608
  254.1 28.1 %slice-start.5 = ((s8[28311552]{0:T(1024)(128)(4,1)}), s8[4194304]{0:T(1024)(128)(4,1)S(1)}, s32[]{:S(2)}) async-start(s8[28311552]{0:T(1024)(128)(4,1)} %bitcast.30), calls=%async_computation.13 | async-start | bytes 8388608
  254.2 28.1 %slice-start.6 = ((s8[28311552]{0:T(1024)(128)(4,1)}), s8[3145728]{0:T(1024)(128)(4,1)S(1)}, s32[]{:S(2)}) async-start(s8[28311552]{0:T(1024)(128)(4,1)} %bitcast.30), calls=%async_computation.14 | async-start | bytes 6291456
  395.4 47.1 %copy-start.2 = (f32[384,768]{1,0:T(8,128)S(1)}, f32[384,768]{1,0:T(8,128)}, u32[]{:S(2)}) copy-start(f32[384,768]{1,0:T(8,128)} %param.4) | copy-start | bytes 3538948
  395.4 87.1 %all-gather.5.cloned.1.call-start = ((), (), s32[]{:S(2)}) async-start(), calls=%async_computation.5 | async-start | bytes 5898240 | tf_op jit(solution)/shard_map/all_gather | solution.py:16
  445.0 214.4 %all-reduce.5.cloned.1.call-start = ((), (), s32[]{:S(2)}) async-start(), calls=%async_computation.6 | async-start | bytes 9437184 | tf_op jit(solution)/shard_map/psum | solution.py:12
  487.4 380.9 %reduce-scatter.5.cloned.1.call-start = ((), (), s32[]{:S(2)}) async-start(), calls=%async_computation.7 | async-start | bytes 5898240 | tf_op jit(solution)/shard_map/reduce_scatter | solution.py:20
  659.4 27.4 %copy-start = (f32[1536,768]{1,0:T(8,128)S(1)}, f32[1536,768]{1,0:T(8,128)}, u32[]{:S(2)}) copy-start(f32[1536,768]{1,0:T(8,128)} %all-reduce.5.cloned.1.call-done) | copy-start | bytes 14155780
  659.4 54.8 %slice-start.9 = ((s8[4718592]{0:T(1024)(128)(4,1)}), s8[4194304]{0:T(1024)(128)(4,1)S(1)}, s32[]{:S(2)}) async-start(s8[4718592]{0:T(1024)(128)(4,1)} %bitcast.34), calls=%async_computation.17 | async-start | bytes 8388608
  686.8 27.3 %slice-start.10 = ((s8[4718592]{0:T(1024)(128)(4,1)}), s8[524288]{0:T(1024)(128)(4,1)S(1)}, s32[]{:S(2)}) async-start(s8[4718592]{0:T(1024)(128)(4,1)} %bitcast.34), calls=%async_computation.18 | async-start | bytes 1048576
  821.2 47.1 %copy-start.1 = (f32[384,768]{1,0:T(8,128)S(1)}, f32[384,768]{1,0:T(8,128)}, u32[]{:S(2)}) copy-start(f32[384,768]{1,0:T(8,128)} %sub.8) | copy-start | bytes 3538948
Sparse Core Ops, SparseCore 0:
  8.9 40.1 all-gather.2
  54.0 171.8 all-reduce.2
  395.5 46.9 reduce-scatter.2
  445.1 37.4 all-gather.4
  487.5 171.8 all-reduce.4
  821.4 46.9 reduce-scatter.4
where the time goes:
time: 886 us; the launch traced here: 878 us
  waiting for transfers between devices  517 us (58%)
  matrix products  331 us (37%)
  other arithmetic  14.5 us (2%)
  between operations  13.9 us (2%)
    psum x2, waiting for transfers between devices, from_root(): return lax.psum(block, axis)  343 us
    dot_general x6, matrix products, body(): jnp.dot(green * screened[t], columns, precision=lax.Precision.HIGHEST, pr...  166 us
    dot_general x6, matrix products, body(): lax.dot_general(rows * green_weight[t], columns, (((1,), (1,)), ((), ()))...  165 us
    reduce_scatter x2, waiting for transfers between devices, scatter_rows(): lax.psum_scatter(partial_value, 'col', scatter_dimension=0, tiled=True)  94.1 us
    all_gather x2, waiting for transfers between devices, gather_rows(): return lax.all_gather(shard, 'col', axis=0, tiled=True)  79.3 us
  transfers between devices with their start and end apart: 6, of which 6 were waited for; matrix products, arithmetic and copies ran while one was open for 0% of the time, Pallas kernels for 0%

commit v1 on v0

--- a/solution.py
+++ b/solution.py
@@ -1,3 +1,4 @@
+import functools
 import jax
 import jax.numpy as jnp
 from jax import lax
@@ -7,13 +8,34 @@
 PASSES = 2
 
 
+def make_sizes(message, array_dim):
+    carry_in = list(message.shape[1:])
+    carry_in[array_dim] *= message.shape[0]
+    return jnp.moveaxis(message, 0, array_dim).reshape(carry_in)
+
+
+def push_the_sizes(frame, peer_axis, join_dim):
+    ndev = lax.psum(1, axis_name=peer_axis)
+    blocks_here = [frame]
+    views = [(no, (no + 1) % ndev) for no in range(ndev)]
+    while len(blocks_here) < ndev:
+        blocks_here.append(lax.ppermute(blocks_here[-1], perm=views, axis_name=peer_axis))
+    outer = lax.axis_index(peer_axis)
+    s_next = jnp.stack(blocks_here, axis=0)
+    blocks_here = s_next[(outer - jnp.arange(ndev)) % ndev]
+    return make_sizes(blocks_here, join_dim)
+
+
+extend_keys = functools.partial(push_the_sizes, peer_axis="col", join_dim=0)
+
+
 def from_root(block, axis, owner):
     block = jnp.where(lax.axis_index(axis) == owner, block, jnp.zeros_like(block))
     return lax.psum(block, axis)
 
 
 def gather_rows(shard):
-    return lax.all_gather(shard, "col", axis=0, tiled=True)
+    return extend_keys(shard)
 
 
 def scatter_rows(partial_value):

time: 886 us -> 928 us (1.047)
  waiting for transfers between devices: 517 us -> 532 us
  other arithmetic: 14.5 us -> 28.1 us
  local copies, waits for them, and re-layouts: 1.3 us -> 12.9 us
    ppermute x0 -> x6, waiting for transfers between devices: none -> 93.2 us  [push_the_sizes(): lax.ppermute(blocks_here[-1], perm=views, axis_name=peer_axis)]
    all_gather x2 -> x0, waiting for transfers between devices: 79.3 us -> none  [gather_rows(): return lax.all_gather(shard, 'col', axis=0, tiled=True)]
    mul x0 -> x2, other arithmetic: none -> 18 us  [body(): rows * green_weight[t]]
    gather x0 -> x2, local copies, waits for them, and re-layouts: none -> 10.7 us  [push_the_sizes(): blocks_here = s_next[(outer - jnp.arange(ndev)) % ndev]]
    select_n x2 -> x1, other arithmetic: 9.63 us -> 0.01 us  [push_the_sizes(): blocks_here = s_next[(outer - jnp.arange(ndev)) % ndev]]
  transfers between devices with their start and end apart: 6 -> 10, of which waited for: 6 -> 10; matrix products, arithmetic and copies ran while one was open for 0% -> 0% of each run, Pallas kernels for 0% -> 0%
where the time goes in v1:
time: 928 us; the launch traced here: 921 us
  waiting for transfers between devices  532 us (57%)
  matrix products  333 us (36%)
  other arithmetic  28.1 us (3%)
  between operations  13.8 us (1%)
  local copies, waits for them, and re-layouts  12.9 us (1%)
    psum x2, waiting for transfers between devices, from_root(): return lax.psum(block, axis)  345 us
    dot_general x6, matrix products, body(): jnp.dot(green * screened[t], columns, precision=lax.Precision.HIGHEST, pr...  168 us
    dot_general x6, matrix products, body(): lax.dot_general(rows * green_weight[t], columns, (((1,), (1,)), ((), ()))...  165 us
    reduce_scatter x2, waiting for transfers between devices, scatter_rows(): lax.psum_scatter(partial_value, 'col', scatter_dimension=0, tiled=True)  94.1 us
    ppermute x6, waiting for transfers between devices, push_the_sizes(): lax.ppermute(blocks_here[-1], perm=views, axis_name=peer_axis)  93.2 us
  transfers between devices with their start and end apart: 10, of which 10 were waited for; matrix products, arithmetic and copies ran while one was open for 0% of the time, Pallas kernels for 0%

profile of v1, /device:TPU:0, one launch (start us, length us, event | category | flops | bytes accessed | tf_op | source)
XLA Modules:
  0.0 921.1 jit_solution(10202379554436037249)
XLA Ops:
  7.0 16.0 %collective-permute-done = f32[384,768]{1,0:T(8,128)S(1)} collective-permute-done((f32[384,768]{1,0:T(8,128)}, f32[384,768]{1,0:T(8,128)S(1)}, u32[]{:S(2)}, u32[]{:S(2)}) %collective-permute-start) | collective-permute-done | bytes 1179680 | tf_op jit(solution)/shard_map/ppermute | solution.py:22
  23.1 15.6 %collective-permute-done.1 = f32[384,768]{1,0:T(8,128)S(1)} collective-permute-done((f32[384,768]{1,0:T(8,128)S(1)}, f32[384,768]{1,0:T(8,128)S(1)}, u32[]{:S(2)}, u32[]{:S(2)}) %collective-permute-start.1) | collective-permute-done | bytes 1179680 | tf_op jit(solution)/shard_map/ppermute | solution.py:22
  39.6 14.7 %collective-permute-done.2 = f32[384,768]{1,0:T(8,128)S(1)} collective-permute-done((f32[384,768]{1,0:T(8,128)S(1)}, f32[384,768]{1,0:T(8,128)S(1)}, u32[]{:S(2)}, u32[]{:S(2)}) %collective-permute-start.2) | collective-permute-done | bytes 1179680 | tf_op jit(solution)/shard_map/ppermute | solution.py:22
  63.4 9.0 bitcast_multiply_fusion.3
  73.7 172.9 %all-reduce.3.cloned.1.call-done = f32[1536,768]{1,0:T(8,128)} async-done(((f32[1536,768]{1,0:T(8,128)}), f32[1536,768]{1,0:T(8,128)}) %all-reduce.3.cloned.1.call-update) | async-done | bytes 4718608 | tf_op jit(solution)/shard_map/psum | solution.py:34
  246.6 28.3 %convolution_multiply_fusion.4 = f32[1536,1536]{1,0:T(8,128)} fusion(f32[1536,768]{1,0:T(8,128)} %get-tuple-element.14, f32[1536,768]{1,0:T(8,128)} %all-reduce.3.cloned.1.call-done, f32[3,1536,1536]{2,1,0:T(8,128)} %param.5), kind=kOutput, calls=%fused_computation.6 | convolution fusion | flops 21745631232 | bytes 28311552 | tf_op jit(solution)/shard_map/dot_general | solution.py:60
  274.9 27.0 %fusion.4 = f32[1536,768]{1,0:T(8,128)} fusion(f32[1536,1536]{1,0:T(8,128)} %convolution_multiply_fusion.4, f32[1536,768]{1,0:T(8,128)S(1)} %copy-done), kind=kOutput, calls=%fused_computation.32 | convolution fusion | flops 21743271936 | bytes 18874368 | tf_op jit(solution)/shard_map/dot_general | solution.py:67
  302.0 27.2 %convolution_multiply_fusion.5 = f32[1536,1536]{1,0:T(8,128)} fusion(f32[1536,768]{1,0:T(8,128)} %get-tuple-element.15, f32[1536,768]{1,0:T(8,128)S(1)} %copy-done, f32[3,1536,1536]{2,1,0:T(8,128)S(1)} %bitcast.57), kind=kOutput, calls=%fused_computation.7 | convolution fusion | flops 21745631232 | bytes 28311552 | tf_op jit(solution)/shard_map/dot_general | solution.py:60
  329.1 27.1 %fusion.3 = f32[1536,768]{1,0:T(8,128)} fusion(f32[1536,1536]{1,0:T(8,128)} %convolution_multiply_fusion.5, f32[1536,768]{1,0:T(8,128)S(1)} %copy-done), kind=kOutput, calls=%fused_computation.31 | convolution fusion | flops 21743271936 | bytes 18874368 | tf_op jit(solution)/shard_map/dot_general | solution.py:67
  356.2 27.1 %convolution_multiply_fusion.3 = f32[1536,1536]{1,0:T(8,128)} fusion(f32[1536,768]{1,0:T(8,128)} %get-tuple-element.12, f32[1536,768]{1,0:T(8,128)S(1)} %copy-done, f32[3,1536,1536]{2,1,0:T(8,128)S(1)} %bitcast.57), kind=kOutput, calls=%fused_computation.5 | convolution fusion | flops 21745631232 | bytes 28311552 | tf_op jit(solution)/shard_map/dot_general | solution.py:60
  383.3 29.9 %multiply_add_fusion.1 = f32[1536,768]{1,0:T(8,128)} fusion(f32[1536,768]{1,0:T(8,128)} %fusion.4, f32[1536,768]{1,0:T(8,128)} %fusion.3, f32[1536,1536]{1,0:T(8,128)} %convolution_multiply_fusion.3, f32[1536,768]{1,0:T(8,128)S(1)} %copy-done, f32[]{:T(128)} %bitcast.10, f32[]{:T(128)} %bitcast.8, f32[]{:T(128)} %bitcast), kind=kOutput, calls=%fused_computation.19 | convolution fusion | flops 21749170176 | bytes 28311564 | tf_op jit(solution)/shard_map/dot_general | solution.py:67
  413.2 47.0 %reduce-scatter.3.cloned.1.call-done = f32[384,768]{1,0:T(8,128)} async-done(((f32[1536,768]{1,0:T(8,128)}), f32[384,768]{1,0:T(8,128)}) %reduce-scatter.3.cloned.1.call-update) | async-done | bytes 1179664 | tf_op jit(solution)/shard_map/reduce_scatter | solution.py:42
  461.7 15.6 %collective-permute-done.3 = f32[384,768]{1,0:T(8,128)S(1)} collective-permute-done((f32[384,768]{1,0:T(8,128)S(1)}, f32[384,768]{1,0:T(8,128)S(1)}, u32[]{:S(2)}, u32[]{:S(2)}) %collective-permute-start.3) | collective-permute-done | bytes 1179680 | tf_op jit(solution)/shard_map/ppermute | solution.py:22
  477.4 15.6 %collective-permute-done.4 = f32[384,768]{1,0:T(8,128)S(1)} collective-permute-done((f32[384,768]{1,0:T(8,128)S(1)}, f32[384,768]{1,0:T(8,128)S(1)}, u32[]{:S(2)}, u32[]{:S(2)}) %collective-permute-start.4) | collective-permute-done | bytes 1179680 | tf_op jit(solution)/shard_map/ppermute | solution.py:22
  493.0 15.6 %collective-permute-done.5 = f32[384,768]{1,0:T(8,128)S(1)} collective-permute-done((f32[384,768]{1,0:T(8,128)S(1)}, f32[384,768]{1,0:T(8,128)S(1)}, u32[]{:S(2)}, u32[]{:S(2)}) %collective-permute-start.5) | collective-permute-done | bytes 1179680 | tf_op jit(solution)/shard_map/ppermute | solution.py:22
  516.4 9.0 bitcast_multiply_fusion
  525.5 172.1 %all-reduce.5.cloned.1.call-done = f32[1536,768]{1,0:T(8,128)} async-done(((f32[1536,768]{1,0:T(8,128)}), f32[1536,768]{1,0:T(8,128)}) %all-reduce.5.cloned.1.call-update) | async-done | bytes 4718608 | tf_op jit(solution)/shard_map/psum | solution.py:34
  697.6 28.5 %convolution_multiply_fusion.1 = f32[1536,1536]{1,0:T(8,128)} fusion(f32[1536,768]{1,0:T(8,128)} %get-tuple-element.10, f32[1536,768]{1,0:T(8,128)} %all-reduce.5.cloned.1.call-done, f32[3,1536,1536]{2,1,0:T(8,128)} %param.5), kind=kOutput, calls=%fused_computation.3 | convolution fusion | flops 21745631232 | bytes 28311552 | tf_op jit(solution)/shard_map/dot_general | solution.py:60
  726.1 27.4 %fusion.6 = f32[1536,768]{1,0:T(8,128)} fusion(f32[1536,1536]{1,0:T(8,128)} %convolution_multiply_fusion.1, f32[1536,768]{1,0:T(8,128)S(1)} %copy-done.1), kind=kOutput, calls=%fused_computation.34 | convolution fusion | flops 21743271936 | bytes 18874368 | tf_op jit(solution)/shard_map/dot_general | solution.py:67
  753.6 27.1 %convolution_multiply_fusion.2 = f32[1536,1536]{1,0:T(8,128)} fusion(f32[1536,768]{1,0:T(8,128)} %get-tuple-element.11, f32[1536,768]{1,0:T(8,128)S(1)} %copy-done.1, f32[3,1536,1536]{2,1,0:T(8,128)S(1)} %bitcast.59), kind=kOutput, calls=%fused_computation.4 | convolution fusion | flops 21745631232 | bytes 28311552 | tf_op jit(solution)/shard_map/dot_general | solution.py:60
  780.6 26.8 %fusion.5 = f32[1536,768]{1,0:T(8,128)} fusion(f32[1536,1536]{1,0:T(8,128)} %convolution_multiply_fusion.2, f32[1536,768]{1,0:T(8,128)S(1)} %copy-done.1), kind=kOutput, calls=%fused_computation.33 | convolution fusion | flops 21743271936 | bytes 18874368 | tf_op jit(solution)/shard_map/dot_general | solution.py:67
  807.5 27.1 %convolution_multiply_fusion = f32[1536,1536]{1,0:T(8,128)} fusion(f32[1536,768]{1,0:T(8,128)} %get-tuple-element.8, f32[1536,768]{1,0:T(8,128)S(1)} %copy-done.1, f32[3,1536,1536]{2,1,0:T(8,128)S(1)} %bitcast.59), kind=kOutput, calls=%fused_computation.2 | convolution fusion | flops 21745631232 | bytes 28311552 | tf_op jit(solution)/shard_map/dot_general | solution.py:60
  834.6 30.0 %multiply_add_fusion = f32[1536,768]{1,0:T(8,128)} fusion(f32[1536,768]{1,0:T(8,128)} %fusion.6, f32[1536,768]{1,0:T(8,128)} %fusion.5, f32[1536,1536]{1,0:T(8,128)} %convolution_multiply_fusion, f32[1536,768]{1,0:T(8,128)S(1)} %copy-done.1, f32[]{:T(128)} %bitcast.10, f32[]{:T(128)} %bitcast.8, f32[]{:T(128)} %bitcast), kind=kOutput, calls=%fused_computation.18 | convolution fusion | flops 21749170176 | bytes 28311564 | tf_op jit(solution)/shard_map/dot_general | solution.py:67
  864.6 47.1 %reduce-scatter.5.cloned.1.call-done = f32[384,768]{1,0:T(8,128)} async-done(((f32[1536,768]{1,0:T(8,128)}), f32[384,768]{1,0:T(8,128)}) %reduce-scatter.5.cloned.1.call-update) | async-done | bytes 1179664 | tf_op jit(solution)/shard_map/reduce_scatter | solution.py:42
  (66 shorter events, 23.7 us)
Async XLA Ops:
  6.5 240.0 %all-reduce.3.cloned.1.call-start = ((), (), s32[]{:S(2)}) async-start(), calls=%async_computation.2 | async-start | bytes 9437184 | tf_op jit(solution)/shard_map/psum | solution.py:34
  6.5 16.5 %collective-permute-start = (f32[384,768]{1,0:T(8,128)}, f32[384,768]{1,0:T(8,128)S(1)}, u32[]{:S(2)}, u32[]{:S(2)}) collective-permute-start(f32[384,768]{1,0:T(8,128)} %param.4), channel_id=1, source_target_pairs={{0,1},{1,2},{2,3},{3,0},{4,5},{5,6},{6,7},{7,4},{8,9},{9,10},{10,1... | collective-permute-start | bytes 3538952 | tf_op jit(solution)/shard_map/ppermute | solution.py:22
  23.0 15.6 %collective-permute-start.1 = (f32[384,768]{1,0:T(8,128)S(1)}, f32[384,768]{1,0:T(8,128)S(1)}, u32[]{:S(2)}, u32[]{:S(2)}) collective-permute-start(f32[384,768]{1,0:T(8,128)S(1)} %collective-permute-done), channel_id=1, source_target_pairs={{0,1},{1,2},{2,3},{3,0},{4,5},{5,6},{6,7},{7,4},{8,9},{9,10},{10,1... | collective-permute-start | bytes 3538952 | tf_op jit(solution)/shard_map/ppermute | solution.py:22
  38.7 15.6 %collective-permute-start.2 = (f32[384,768]{1,0:T(8,128)S(1)}, f32[384,768]{1,0:T(8,128)S(1)}, u32[]{:S(2)}, u32[]{:S(2)}) collective-permute-start(f32[384,768]{1,0:T(8,128)S(1)} %collective-permute-done.1), channel_id=1, source_target_pairs={{0,1},{1,2},{2,3},{3,0},{4,5},{5,6},{6,7},{7,4},{8,9},{9,10},{10,1... | collective-permute-start | bytes 3538952 | tf_op jit(solution)/shard_map/ppermute | solution.py:22
  72.4 387.8 %reduce-scatter.3.cloned.1.call-start = ((), (), s32[]{:S(2)}) async-start(), calls=%async_computation.3 | async-start | bytes 5898240 | tf_op jit(solution)/shard_map/reduce_scatter | solution.py:42
  246.6 28.3 %copy-start = (f32[1536,768]{1,0:T(8,128)S(1)}, f32[1536,768]{1,0:T(8,128)}, u32[]{:S(2)}) copy-start(f32[1536,768]{1,0:T(8,128)} %all-reduce.3.cloned.1.call-done) | copy-start | bytes 14155780
  246.6 55.3 %slice-start = ((s8[28311552]{0:T(1024)(128)(4,1)}), s8[4194304]{0:T(1024)(128)(4,1)S(1)}, s32[]{:S(2)}) async-start(s8[28311552]{0:T(1024)(128)(4,1)} %bitcast.56), calls=%async_computation.6 | async-start | bytes 8388608
  246.6 55.3 %slice-start.1 = ((s8[28311552]{0:T(1024)(128)(4,1)}), s8[4194304]{0:T(1024)(128)(4,1)S(1)}, s32[]{:S(2)}) async-start(s8[28311552]{0:T(1024)(128)(4,1)} %bitcast.56), calls=%async_computation.7 | async-start | bytes 8388608
  246.6 55.3 %slice-start.2 = ((s8[28311552]{0:T(1024)(128)(4,1)}), s8[4194304]{0:T(1024)(128)(4,1)S(1)}, s32[]{:S(2)}) async-start(s8[28311552]{0:T(1024)(128)(4,1)} %bitcast.56), calls=%async_computation.8 | async-start | bytes 8388608
  246.6 55.4 %slice-start.3 = ((s8[28311552]{0:T(1024)(128)(4,1)}), s8[4194304]{0:T(1024)(128)(4,1)S(1)}, s32[]{:S(2)}) async-start(s8[28311552]{0:T(1024)(128)(4,1)} %bitcast.56), calls=%async_computation.9 | async-start | bytes 8388608
  413.2 47.1 %copy-start.4 = (f32[384,768]{1,0:T(8,128)S(1)}, f32[384,768]{1,0:T(8,128)}, u32[]{:S(2)}) copy-start(f32[384,768]{1,0:T(8,128)} %param.4) | copy-start | bytes 3538948
  413.2 284.4 %all-reduce.5.cloned.1.call-start = ((), (), s32[]{:S(2)}) async-start(), calls=%async_computation.4 | async-start | bytes 9437184 | tf_op jit(solution)/shard_map/psum | solution.py:34
  461.7 47.0 %copy-start.2 = (f32[384,768]{1,0:T(8,128)}, f32[384,768]{1,0:T(8,128)S(1)}, u32[]{:S(2)}) copy-start(f32[384,768]{1,0:T(8,128)S(1)} %sub.25) | copy-start | bytes 3538948
  461.7 15.7 %collective-permute-start.3 = (f32[384,768]{1,0:T(8,128)S(1)}, f32[384,768]{1,0:T(8,128)S(1)}, u32[]{:S(2)}, u32[]{:S(2)}) collective-permute-start(f32[384,768]{1,0:T(8,128)S(1)} %sub.25), channel_id=1, source_target_pairs={{0,1},{1,2},{2,3},{3,0},{4,5},{5,6},{6,7},{7,4},{8,9},{9,10},{10,1... | collective-permute-start | bytes 3538952 | tf_op jit(solution)/shard_map/ppermute | solution.py:22
  477.4 15.6 %collective-permute-start.4 = (f32[384,768]{1,0:T(8,128)S(1)}, f32[384,768]{1,0:T(8,128)S(1)}, u32[]{:S(2)}, u32[]{:S(2)}) collective-permute-start(f32[384,768]{1,0:T(8,128)S(1)} %collective-permute-done.3), channel_id=1, source_target_pairs={{0,1},{1,2},{2,3},{3,0},{4,5},{5,6},{6,7},{7,4},{8,9},{9,10},{10,1... | collective-permute-start | bytes 3538952 | tf_op jit(solution)/shard_map/ppermute | solution.py:22
  493.0 15.6 %collective-permute-start.5 = (f32[384,768]{1,0:T(8,128)S(1)}, f32[384,768]{1,0:T(8,128)S(1)}, u32[]{:S(2)}, u32[]{:S(2)}) collective-permute-start(f32[384,768]{1,0:T(8,128)S(1)} %collective-permute-done.4), channel_id=1, source_target_pairs={{0,1},{1,2},{2,3},{3,0},{4,5},{5,6},{6,7},{7,4},{8,9},{9,10},{10,1... | collective-permute-start | bytes 3538952 | tf_op jit(solution)/shard_map/ppermute | solution.py:22
  525.5 386.2 %reduce-scatter.5.cloned.1.call-start = ((), (), s32[]{:S(2)}) async-start(), calls=%async_computation.5 | async-start | bytes 5898240 | tf_op jit(solution)/shard_map/reduce_scatter | solution.py:42
  697.6 28.6 %copy-start.1 = (f32[1536,768]{1,0:T(8,128)S(1)}, f32[1536,768]{1,0:T(8,128)}, u32[]{:S(2)}) copy-start(f32[1536,768]{1,0:T(8,128)} %all-reduce.5.cloned.1.call-done) | copy-start | bytes 14155780
  697.6 55.9 %slice-start.7 = ((s8[28311552]{0:T(1024)(128)(4,1)}), s8[4194304]{0:T(1024)(128)(4,1)S(1)}, s32[]{:S(2)}) async-start(s8[28311552]{0:T(1024)(128)(4,1)} %bitcast.58), calls=%async_computation.13 | async-start | bytes 8388608
  697.6 55.9 %slice-start.8 = ((s8[28311552]{0:T(1024)(128)(4,1)}), s8[4194304]{0:T(1024)(128)(4,1)S(1)}, s32[]{:S(2)}) async-start(s8[28311552]{0:T(1024)(128)(4,1)} %bitcast.58), calls=%async_computation.14 | async-start | bytes 8388608
  697.6 55.9 %slice-start.9 = ((s8[28311552]{0:T(1024)(128)(4,1)}), s8[4194304]{0:T(1024)(128)(4,1)S(1)}, s32[]{:S(2)}) async-start(s8[28311552]{0:T(1024)(128)(4,1)} %bitcast.58), calls=%async_computation.15 | async-start | bytes 8388608
  697.6 55.9 %slice-start.10 = ((s8[28311552]{0:T(1024)(128)(4,1)}), s8[4194304]{0:T(1024)(128)(4,1)S(1)}, s32[]{:S(2)}) async-start(s8[28311552]{0:T(1024)(128)(4,1)} %bitcast.58), calls=%async_computation.16 | async-start | bytes 8388608
  726.1 27.4 %slice-start.13 = ((s8[28311552]{0:T(1024)(128)(4,1)}), s8[3145728]{0:T(1024)(128)(4,1)S(1)}, s32[]{:S(2)}) async-start(s8[28311552]{0:T(1024)(128)(4,1)} %bitcast.58), calls=%async_computation.19 | async-start | bytes 6291456
  864.6 47.1 %copy-start.3 = (f32[384,768]{1,0:T(8,128)S(1)}, f32[384,768]{1,0:T(8,128)}, u32[]{:S(2)}) copy-start(f32[384,768]{1,0:T(8,128)} %copy-done.2) | copy-start | bytes 3538948
  (6 other events, 136.6 us)
Sparse Core Ops, SparseCore 0:
  72.5 174.0 all-reduce.2
  413.3 46.8 reduce-scatter.2
  525.6 171.9 all-reduce.4
  864.7 46.9 reduce-scatter.4
